TPU v7x, 32 devices: a whole 2x2x4 slice. The times are simulated.
32 devices in a mesh: dp: 8 (over y, x, core), mp: 4 (over z).
Axes of the slice: x: 2, y: 2, z: 4, core: 2. Of those that a mesh axis runs over, the one named last changes fastest.
Arguments:
- activations: bfloat16 [128, 288, 768], P(('dp', 'mp')), may hold values from -2.5 to 2.5
- cotangent: bfloat16 [128, 288, 768], P(('dp', 'mp')), may hold values from -2.5 to 2.5
- segments: int32 [128, 288], P('dp'), may hold values from 0 to 2, never falling along the last dimension, each value on 1 to 160 neighbouring positions
- triple_weight: bfloat16 [3, 768, 768], P(None, None, 'mp'), may hold values from -0.21875 to 0.21875
- query_value_bias: bfloat16 [2, 12, 64], P(None, 'mp'), may hold values from -1.5 to 1.5
- output_weight: bfloat16 [768, 768], P('mp'), may hold values from -0.875 to 0.875
- expand_weight: bfloat16 [768, 3072], P(None, 'mp'), may hold values from -0.21875 to 0.21875
- expand_bias: bfloat16 [48, 64], P('mp'), may hold values from -1.5 to 1.5
- shrink_weight: bfloat16 [3072, 768], P('mp'), may hold values from -0.109375 to 0.109375
- vector_params: bfloat16 [6, 768], replicated
- triple_master: float32 [3, 768, 768], P(None, 'dp', 'mp'), may hold values from -0.21875 to 0.21875
- triple_first: float32 [3, 768, 768], P(None, 'dp', 'mp'), may hold values from -144 to 144
- triple_second: float32 [3, 768, 768], P(None, 'dp', 'mp'), may hold values from 2211.84 to 8847.36
- query_value_master: float32 [2, 12, 64], P(None, 'mp', 'dp'), may hold values from -1.5 to 1.5
- query_value_first: float32 [2, 12, 64], P(None, 'mp', 'dp'), may hold values from -192 to 192
- query_value_second: float32 [2, 12, 64], P(None, 'mp', 'dp'), may hold values from 3944.448 to 15851.52
- output_master: float32 [768, 768], P('mp', 'dp'), may hold values from -0.875 to 0.875
- output_first: float32 [768, 768], P('mp', 'dp'), may hold values from -57.6 to 57.6
- output_second: float32 [768, 768], P('mp', 'dp'), may hold values from 353.8944 to 1400.832
- expand_master: float32 [768, 3072], P('dp', 'mp'), may hold values from -0.21875 to 0.21875
- expand_first: float32 [768, 3072], P('dp', 'mp'), may hold values from -96 to 96
- expand_second: float32 [768, 3072], P('dp', 'mp'), may hold values from 995.328 to 3944.448
- expand_bias_master: float32 [48, 64], P('mp', 'dp'), may hold values from -1.5 to 1.5
- expand_bias_first: float32 [48, 64], P('mp', 'dp'), may hold values from -96 to 96
- expand_bias_second: float32 [48, 64], P('mp', 'dp'), may hold values from 995.328 to 3944.448
- shrink_master: float32 [3072, 768], P('mp', 'dp'), may hold values from -0.109375 to 0.109375
- shrink_first: float32 [3072, 768], P('mp', 'dp'), may hold values from -192 to 192
- shrink_second: float32 [3072, 768], P('mp', 'dp'), may hold values from 3944.448 to 15851.52
- vector_master: float32 [6, 768], P(None, ('dp', 'mp'))
- vector_first: float32 [6, 768], P(None, ('dp', 'mp')), may hold values from -384 to 384
- vector_second: float32 [6, 768], P(None, ('dp', 'mp')), may hold values from 15851.52 to 62668.8
Outputs:
- block_output: bfloat16 [128, 288, 768], P(('dp', 'mp'))
- input_grad: float32 [128, 288, 768], P(('dp', 'mp'))
- triple_master_new: float32 [3, 768, 768], P(None, 'dp', 'mp')
- triple_first_new: float32 [3, 768, 768], P(None, 'dp', 'mp')
- triple_second_new: float32 [3, 768, 768], P(None, 'dp', 'mp')
- triple_copy: bfloat16 [3, 768, 768], P(None, 'dp', 'mp')
- query_value_master_new: float32 [2, 12, 64], P(None, 'mp', 'dp')
- query_value_first_new: float32 [2, 12, 64], P(None, 'mp', 'dp')
- query_value_second_new: float32 [2, 12, 64], P(None, 'mp', 'dp')
- query_value_copy: bfloat16 [2, 12, 64], P(None, 'mp', 'dp')
- output_master_new: float32 [768, 768], P('mp', 'dp')
- output_first_new: float32 [768, 768], P('mp', 'dp')
- output_second_new: float32 [768, 768], P('mp', 'dp')
- output_copy: bfloat16 [768, 768], P('mp', 'dp')
- expand_master_new: float32 [768, 3072], P('dp', 'mp')
- expand_first_new: float32 [768, 3072], P('dp', 'mp')
- expand_second_new: float32 [768, 3072], P('dp', 'mp')
- expand_copy: bfloat16 [768, 3072], P('dp', 'mp')
- expand_bias_master_new: float32 [48, 64], P('mp', 'dp')
- expand_bias_first_new: float32 [48, 64], P('mp', 'dp')
- expand_bias_second_new: float32 [48, 64], P('mp', 'dp')
- expand_bias_copy: bfloat16 [48, 64], P('mp', 'dp')
- shrink_master_new: float32 [3072, 768], P('mp', 'dp')
- shrink_first_new: float32 [3072, 768], P('mp', 'dp')
- shrink_second_new: float32 [3072, 768], P('mp', 'dp')
- shrink_copy: bfloat16 [3072, 768], P('mp', 'dp')
- vector_master_new: float32 [6, 768], P(None, ('dp', 'mp'))
- vector_first_new: float32 [6, 768], P(None, ('dp', 'mp'))
- vector_second_new: float32 [6, 768], P(None, ('dp', 'mp'))
- vector_copy: bfloat16 [6, 768], P(None, ('dp', 'mp'))
Inputs may be any that keep to these rules, and one draw needn't show every extreme that they name: `segments`: along a row the pair numbers never fall; each pair has 1 to 160 tokens, and each row has one pair of exactly 160.
All inputs are finite; a program needn't handle non-finite values.
Results may differ from a plain program's by a relative error of at most 0.018.
Values may be sent and summed in bfloat16 or wider, within the bound.
A program may use at most 256 MiB of HBM per device.

v0:
```python
import jax
import jax.numpy as jnp
from jax import lax
from jax.sharding import PartitionSpec as P

D = 768
HEAD = 64
FF = 3072
STEP = 10
NORM_EPS = 1e-05
BETA_ONE = 0.5
BETA_TWO = 0.6
ADAM_EPS = 1e-08
WEIGHT_DECAY = 0.01
MASKED = -1e30
SQRT_HALF = 0.7071067811865476
INV_ROOT_TAU = 0.3989422804014327


def norm_forward(summed, gain, shift):
    centre = summed - jnp.mean(summed, axis=-1, keepdims=True)
    scale = lax.rsqrt(jnp.mean(centre * centre, axis=-1, keepdims=True) + NORM_EPS)
    normed = centre * scale
    return (gain * normed + shift, normed, scale)


def norm_backward(gradient, gain, normed, scale):
    scaled = gradient * gain
    centred = scaled - jnp.mean(scaled, axis=-1, keepdims=True)
    return scale * (centred - normed * jnp.mean(scaled * normed, axis=-1, keepdims=True))


def adam_update(master, first, second, gradient, rate):
    first_new = BETA_ONE * first + (1.0 - BETA_ONE) * gradient
    second_new = BETA_TWO * second + (1.0 - BETA_TWO) * gradient * gradient
    corrected = first_new / (1.0 - BETA_ONE**STEP)
    spread = jnp.sqrt(second_new / (1.0 - BETA_TWO**STEP))
    master_new = master - rate * (corrected / (spread + ADAM_EPS) + WEIGHT_DECAY * master)
    return (master_new, first_new, second_new, master_new.astype(jnp.bfloat16))


def gather_weight(shard, rows_axis):
    count = lax.axis_size("dp")
    piece = shard.shape[rows_axis] // count
    own = lax.dynamic_slice_in_dim(shard, lax.axis_index("dp") * piece, piece, rows_axis)
    return own


def mm(a, b, dims):
    return lax.dot_general(a, b, (dims, ((), ())), preferred_element_type=jnp.float32)


def per_device(
    activations,
    cotangent,
    segments,
    triple_weight,
    query_value_bias,
    output_weight,
    expand_weight,
    expand_bias,
    shrink_weight,
    vector_params,
    *state
):
    rows, length, _ = activations.shape
    tokens = rows * length
    triple = gather_weight(triple_weight, 1)
    triple = lax.all_gather(
        lax.all_gather(triple, "mp", axis=2, tiled=True), "dp", axis=1, tiled=True
    )
    output = gather_weight(output_weight, 1)
    output = lax.all_gather(
        lax.all_gather(output, "mp", axis=0, tiled=True), "dp", axis=1, tiled=True
    )
    expand = gather_weight(expand_weight, 0)
    expand = lax.all_gather(
        lax.all_gather(expand, "mp", axis=1, tiled=True), "dp", axis=0, tiled=True
    )
    shrink = gather_weight(shrink_weight, 1)
    shrink = lax.all_gather(
        lax.all_gather(shrink, "mp", axis=0, tiled=True), "dp", axis=1, tiled=True
    )
    biases = (
        lax.all_gather(query_value_bias, "mp", axis=1, tiled=True).reshape(2, D).astype(jnp.float32)
    )
    expand_shift = (
        lax.all_gather(expand_bias, "mp", axis=0, tiled=True).reshape(-1).astype(jnp.float32)
    )
    gains = vector_params.astype(jnp.float32)
    heads = D // HEAD
    seg = lax.dynamic_slice_in_dim(segments, lax.axis_index("mp") * rows, rows, 0)
    allowed = (seg[:, :, None] == seg[:, None, :])[:, None]
    x = activations.reshape(tokens, D)
    back = cotangent.reshape(tokens, D).astype(jnp.float32)

    def split(t):
        return t.reshape(rows, length, heads, HEAD)

    query = (mm(x, triple[0], ((1,), (0,))) + biases[0]).astype(jnp.bfloat16)
    key = mm(x, triple[1], ((1,), (0,))).astype(jnp.bfloat16)
    value = (mm(x, triple[2], ((1,), (0,))) + biases[1]).astype(jnp.bfloat16)
    q4, k4, v4 = (split(query), split(key), split(value))
    scores = jnp.einsum("rqhc,rkhc->rhqk", q4, k4, preferred_element_type=jnp.float32) * HEAD ** (
        -0.5
    )
    scores = jnp.where(allowed, scores, MASKED)
    row_max = jnp.max(scores, axis=-1, keepdims=True)
    weights = jnp.exp(scores - row_max)
    probs = weights / jnp.sum(weights, axis=-1, keepdims=True)
    probs_low = probs.astype(jnp.bfloat16)
    context = jnp.einsum("rhqk,rkhc->rqhc", probs_low, v4, preferred_element_type=jnp.float32)
    context = context.astype(jnp.bfloat16).reshape(tokens, D)
    attended = mm(context, output, ((1,), (0,)))
    mixed = x.astype(jnp.float32) + attended + gains[2]
    hidden, normed_one, scale_one = norm_forward(mixed, gains[0], gains[1])
    hidden_low = hidden.astype(jnp.bfloat16)
    expanded = mm(hidden_low, expand, ((1,), (0,))) + expand_shift
    cumulative = 0.5 * (1.0 + jax.scipy.special.erf(expanded * SQRT_HALF))
    active = (expanded * cumulative).astype(jnp.bfloat16)
    slope = (cumulative + expanded * jnp.exp(-0.5 * expanded * expanded) * INV_ROOT_TAU).astype(
        jnp.bfloat16
    )
    shrunk = mm(active, shrink, ((1,), (0,)))
    summed = hidden + shrunk + gains[5]
    result, normed_two, scale_two = norm_forward(summed, gains[3], gains[4])
    dsummed = norm_backward(back, gains[3], normed_two, scale_two)
    dsummed_low = dsummed.astype(jnp.bfloat16)

    def reduce_grad(part):
        part = part.astype(jnp.bfloat16)
        part = lax.psum_scatter(part, "dp", scatter_dimension=part.ndim - 2, tiled=True)
        return lax.psum_scatter(part, "mp", scatter_dimension=part.ndim - 1, tiled=True).astype(
            jnp.float32
        )

    shrink_grad = reduce_grad(mm(dsummed_low, active, ((0,), (0,))))
    dactive = mm(dsummed_low, shrink, ((1,), (1,)))
    dexpanded = (dactive * slope).astype(jnp.bfloat16)
    expand_grad = reduce_grad(mm(hidden_low, dexpanded, ((0,), (0,))))
    dhidden = dsummed + mm(dexpanded, expand, ((1,), (1,)))
    dmixed = norm_backward(dhidden, gains[0], normed_one, scale_one)
    dmixed_low = dmixed.astype(jnp.bfloat16)
    output_grad = reduce_grad(mm(dmixed_low, context, ((0,), (0,))))
    dcontext = split(mm(dmixed_low, output, ((1,), (1,))).astype(jnp.bfloat16))
    dvalue = jnp.einsum("rhqk,rqhc->rkhc", probs_low, dcontext, preferred_element_type=jnp.float32)
    dprobs = jnp.einsum("rqhc,rkhc->rhqk", dcontext, v4, preferred_element_type=jnp.float32)
    inner = jnp.sum(probs * dprobs, axis=-1, keepdims=True)
    dscores = (probs * (dprobs - inner)).astype(jnp.bfloat16)
    dquery = jnp.einsum(
        "rhqk,rkhc->rqhc", dscores, k4, preferred_element_type=jnp.float32
    ) * HEAD ** (-0.5)
    dkey = jnp.einsum(
        "rhqk,rqhc->rkhc", dscores, q4, preferred_element_type=jnp.float32
    ) * HEAD ** (-0.5)
    dthree = [t.astype(jnp.bfloat16).reshape(tokens, D) for t in (dquery, dkey, dvalue)]
    triple_grad = reduce_grad(jnp.stack([mm(x, t, ((0,), (0,))) for t in dthree]))
    input_grad = dmixed
    for j in range(3):
        input_grad = input_grad + mm(dthree[j], triple[j], ((1,), (1,)))

    def total(t):
        return jnp.sum(t.astype(jnp.float32), axis=0)

    vector_grad = jnp.stack(
        [
            total(dhidden * normed_one),
            total(dhidden),
            total(dmixed),
            total(back * normed_two),
            total(back),
            total(dsummed),
            total(dthree[0]),
            total(dthree[2]),
        ]
    )
    vector_grad = lax.psum(
        jnp.concatenate([vector_grad, total(dexpanded).reshape(4, D)]), ("dp", "mp")
    )
    dp, mp = (lax.axis_index("dp"), lax.axis_index("mp"))
    groups, parts = (lax.axis_size("mp"), lax.axis_size("dp"))
    width = D // (groups * parts)
    vec = lax.dynamic_slice_in_dim(vector_grad[:6], (dp * groups + mp) * width, width, 1)
    qv = vector_grad[6:8].reshape(2, heads, HEAD)
    qv = lax.dynamic_slice_in_dim(qv, mp * (heads // groups), heads // groups, 1)
    qv = lax.dynamic_slice_in_dim(qv, dp * (HEAD // parts), HEAD // parts, 2)
    eb = vector_grad[8:].reshape(FF // HEAD, HEAD)
    eb = lax.dynamic_slice_in_dim(eb, mp * (FF // HEAD // groups), FF // HEAD // groups, 0)
    eb = lax.dynamic_slice_in_dim(eb, dp * (HEAD // parts), HEAD // parts, 1)
    grads = (triple_grad, qv, output_grad.T, expand_grad, eb, shrink_grad.T, vec)
    rates = (D ** (-0.5), 0.5, (D // 16) ** (-0.5), D ** (-0.5), 0.5, FF ** (-0.5), 0.3)
    outs = (
        result.astype(jnp.bfloat16).reshape(activations.shape),
        input_grad.reshape(activations.shape),
    )
    for i in range(7):
        outs = outs + adam_update(
            state[3 * i], state[3 * i + 1], state[3 * i + 2], grads[i], rates[i]
        )
    return outs


STATE_SPECS = (
    P(None, "dp", "mp"),
    P(None, "mp", "dp"),
    P("mp", "dp"),
    P("dp", "mp"),
    P("mp", "dp"),
    P("mp", "dp"),
    P(None, ("dp", "mp")),
)


def solution(mesh):
    rows = P(("dp", "mp"), None, None)
    placed = (
        rows,
        rows,
        P("dp", None),
        P(None, None, "mp"),
        P(None, "mp", None),
        P("mp", None),
        P(None, "mp"),
        P("mp", None),
        P("mp", None),
        P(),
    )
    for spec in STATE_SPECS:
        placed = placed + (spec,) * 3
    out_specs = (rows, rows)
    for spec in STATE_SPECS:
        out_specs = out_specs + (spec,) * 4
    return jax.shard_map(
        per_device, mesh=mesh, in_specs=placed, out_specs=out_specs, check_vma=False
    )
```

profile of v0, /device:TPU:0, one launch (start us, length us, event | category | flops | bytes accessed | tf_op | source)
XLA Modules:
  0.0 650.2 jit_solution(2121431900021771325)
XLA Ops:
  8.6 21.7 %all_gather.30 = bf16[3,96,768]{1,0,2:T(4,128)(2,1)} all-gather(bf16[3,96,192]{1,0,2:T(4,128)(2,1)S(1)} %copy.234), channel_id=1, replica_groups=mesh['dp'=8,'mp'=4] {'mp'}, dimensions={2}, use_global_device_ids=true | all-gather | bytes 552960 | tf_op jit(solution)/shard_map/all_gather | solution.py:70
  33.6 13.6 %all_gather.33 = bf16[768,96]{1,0:T(8,128)(2,1)S(1)} all-gather(bf16[192,96]{1,0:T(8,128)(2,1)S(1)} %constant_dynamic-slice_fusion.2), channel_id=1, replica_groups=mesh['dp'=8,'mp'=4] {'mp'}, dimensions={0}, use_global_device_ids=true | all-gather | bytes 184320 | tf_op jit(solution)/shard_map/all_gather | solution.py:74
  48.1 17.4 %all_gather.35 = bf16[96,3072]{1,0:T(8,128)(2,1)} all-gather(bf16[96,768]{1,0:T(8,128)(2,1)S(1)} %constant_dynamic-slice_fusion.1), channel_id=1, replica_groups=mesh['dp'=8,'mp'=4] {'mp'}, dimensions={1}, use_global_device_ids=true | all-gather | bytes 737280 | tf_op jit(solution)/shard_map/all_gather | solution.py:78
  66.9 15.8 %all_gather.38 = bf16[3072,96]{0,1:T(8,128)(2,1)} all-gather(bf16[768,96]{0,1:T(8,128)(2,1)S(1)} %copy.235), channel_id=1, replica_groups=mesh['dp'=8,'mp'=4] {'mp'}, dimensions={0}, use_global_device_ids=true | all-gather | bytes 737280 | tf_op jit(solution)/shard_map/all_gather | solution.py:82
  82.8 11.9 %all_gather.32 = bf16[2,12,64]{2,0,1:T(2,128)(2,1)S(1)} all-gather(bf16[2,3,64]{2,0,1:T(2,128)(2,1)S(1)} %copy-done.35), channel_id=1, replica_groups=mesh['dp'=8,'mp'=4] {'mp'}, dimensions={1}, use_global_device_ids=true | all-gather | bytes 3840 | tf_op jit(solution)/shard_map/all_gather | solution.py:85
  96.0 13.1 %all-gather = bf16[4,12,64]{2,1,0:T(8,128)(2,1)S(1)} all-gather(bf16[1,12,64]{2,1,0:T(8,128)(2,1)S(1)} %bitcast.132), channel_id=1, replica_groups=mesh['dp'=8,'mp'=4] {'mp'}, dimensions={0}, use_global_device_ids=true | all-gather | bytes 7680 | tf_op jit(solution)/shard_map/all_gather | solution.py:88
  110.8 4.9 fusion.27
  115.7 4.8 reshape.182
  120.5 5.6 fusion.29
  126.1 5.7 reshape.183
  131.8 5.0 fusion.28
  136.8 5.6 reshape.181
  142.4 11.9 %fusion.36 = f32[4,12,288,288]{2,3,1,0:T(8,128)} fusion(bf16[4,288,12,64]{1,0,3,2:T(4,128)(2,1)} %reshape.183, bf16[4,288,12,64]{1,0,3,2:T(4,128)(2,1)S(1)} %reshape.182), kind=kOutput, calls=%fused_computation.80 | convolution fusion | flops 509607936 | bytes 19464192 | tf_op jit(solution)/shard_map/rqhc,rkhc->rhqk/dot_general | solution.py:104
  154.3 25.5 %fusion.85 = (f32[4,12,288]{2,1,0:T(8,128)S(1)}, f32[4,12,288,288]{2,3,1,0:T(8,128)}) fusion(f32[4,12,288,288]{2,3,1,0:T(8,128)} %fusion.36, pred[4,288,288]{1,2,0:T(8,128)(4,1)S(1)} %broadcast_compare_fusion), kind=kOutput, calls=%fused_computation.169 | output fusion | flops 23888160 | bytes 32237568 | tf_op jit(solution)/shard_map/sub | solution.py:109
  179.8 9.3 %convert_bitcast_fusion.1 = bf16[4,288,12,64]{1,3,2,0:T(8,128)(2,1)S(1)} fusion(bf16[4,288,12,64]{1,0,3,2:T(4,128)(2,1)S(1)} %copy-done.15, f32[4,12,288,288]{2,3,1,0:T(8,128)} %get-tuple-element.200, f32[4,12,288]{2,1,0:T(8,128)S(1)} %get-tuple-element.199), kind=kOutput, calls=%fused_computation.75 | convolution fusion | flops 518455296 | bytes 19519488 | tf_op jit(solution)/shard_map/rhqk,rkhc->rqhc/dot_general | solution.py:112
  193.6 4.2 fusion.86
  200.3 13.7 %multiply_convert_fusion.1 = (bf16[1152,3072]{1,0:T(8,128)(2,1)}, f32[1152,3072]{1,0:T(8,128)}) fusion(f32[3072]{0:T(1024)S(1)} %reshape.194, bf16[768,3072]{1,0:T(8,128)(2,1)} %all-gather.10.cloned.1.call-done, f32[1152,768]{1,0:T(8,128)} %copy-done.9, f32[768]{0:T(1024)S(1)} %get-tuple-element.161, f32[1152]{0:T(1024)S(1)} %add_rsqrt_fusion.1, ...), kind=kOutput, calls=%fused_computation.14 | convolution fusion | flops 5461475328 | bytes 29518848 | tf_op jit(solution)/shard_map/dot_general | solution.py:50
  214.0 11.8 %fusion.87 = (f32[1152]{0:T(1024)S(1)}, f32[1152,768]{1,0:T(8,128)S(1)}) fusion(f32[768]{0:T(1024)S(1)} %get-tuple-element.160, bf16[1152,3072]{1,0:T(8,128)(2,1)} %get-tuple-element.203, bf16[3072,768]{0,1:T(8,128)(2,1)} %all-gather.12.cloned.1.call-done, f32[768]{0:T(1024)S(1)} %get-tuple-element.161, f32[1152]{0:T(1024)S(1)} %add_rsqrt_fusion.1, ...), kind=kOutput, calls=%fused_computation.171 | convolution fusion | flops 5442010112 | bytes 18897408 | tf_op jit(solution)/shard_map/dot_general | solution.py:50
  232.3 16.6 %convert_reduce_fusion = (f32[3072]{0:T(1024)}, bf16[1152,3072]{1,0:T(8,128)(2,1)}) fusion(f32[1152,3072]{1,0:T(8,128)} %get-tuple-element.204, bf16[3072,768]{0,1:T(8,128)(2,1)S(1)} %copy-done.36, f32[1152,768]{1,0:T(8,128)S(1)} %get-tuple-element.184), kind=kOutput, calls=%fused_computation.13 | convolution fusion | flops 5486244864 | bytes 29503488 | tf_op jit(solution)/shard_map/dot_general | solution.py:50
  249.0 9.7 %multiply_reduce_fusion.1 = (f32[768]{0:T(1024)}, f32[1152]{0:T(1024)S(1)}, f32[1152]{0:T(1024)S(1)}, f32[768]{0:T(1024)}, f32[1152,768]{1,0:T(8,128)S(1)}) fusion(f32[1152,768]{1,0:T(8,128)S(1)} %copy-done.10, f32[1152]{0:T(1024)S(1)} %add_rsqrt_fusion.1, f32[1152]{0:T(1024)S(1)} %broadcast_multiply_fusion.4, f32[768]{0:T(1024)S(1)} %get-tuple-element.163, ...), kind=kOutput, calls=%fused_computation.54 | convolution fusion | flops 5444661248 | bytes 22440960 | tf_op jit(solution)/shard_map/dot_general | solution.py:50
  263.8 4.7 reshape.204
  268.5 6.1 copy.188
  274.6 12.8 %convert_reduce_fusion.1 = (f32[12,64]{1,0:T(8,128)}, bf16[4,288,12,64]{1,3,2,0:T(8,128)(2,1)}) fusion(bf16[4,288,12,64]{1,3,2,0:T(8,128)(2,1)S(1)} %copy.188, f32[4,12,288,288]{2,3,1,0:T(8,128)} %get-tuple-element.200, f32[4,12,288]{2,1,0:T(8,128)S(1)} %get-tuple-element.199), kind=kOutput, calls=%fused_computation.28 | convolution fusion | flops 520224000 | bytes 19522560 | tf_op jit(solution)/shard_map/rhqk,rqhc->rkhc/dot_general | solution.py:146
  287.4 18.2 %multiply_reduce_fusion = (f32[4,12,288]{2,1,0:T(8,128)S(1)}, f32[4,12,288,288]{2,3,1,0:T(8,128)}) fusion(f32[4,12,288,288]{2,3,1,0:T(8,128)} %get-tuple-element.200, f32[4,12,288]{2,1,0:T(8,128)S(1)} %get-tuple-element.199, bf16[4,288,12,64]{1,3,2,0:T(8,128)(2,1)S(1)} %copy.188, bf16[4,288,12,64]{1,0,3,2:T(4,128)(2,1)} %reshape.181), kind=kOutput, calls=%fused_computation.2 | convolution fusion | flops 521538048 | bytes 35500032 | tf_op jit(solution)/shard_map/rqhc,rkhc->rhqk/dot_general | solution.py:147
  305.6 5.3 convolution_convert_fusion.4
  310.9 14.6 %multiply_convert_fusion = bf16[4,12,288,288]{2,3,1,0:T(8,128)(2,1)S(1)} fusion(f32[4,12,288,288]{2,3,1,0:T(8,128)} %get-tuple-element.209, f32[4,12,288]{2,1,0:T(8,128)S(1)} %get-tuple-element.208, f32[4,12,288,288]{2,3,1,0:T(8,128)} %get-tuple-element.200, f32[4,12,288]{2,1,0:T(8,128)S(1)} %get-tuple-element.199), kind=kLoop, calls=%fused_computation.1 | loop fusion | flops 15925248 | bytes 39923712 | tf_op jit(solution)/shard_map/convert_element_type | solution.py:149
  325.6 4.0 copy-done.2
  329.6 3.6 convert_reduce_fusion.2
  333.3 9.4 %fusion.31 = bf16[4,288,12,64]{1,3,2,0:T(8,128)(2,1)} fusion(bf16[4,12,288,288]{2,3,1,0:T(8,128)(2,1)} %copy-done.2, bf16[4,288,12,64]{1,0,3,2:T(4,128)(2,1)S(1)} %copy-done.4), kind=kOutput, calls=%fused_computation.73 | convolution fusion | flops 511377408 | bytes 11501568 | tf_op jit(solution)/shard_map/rhqk,rqhc->rkhc/dot_general | solution.py:153
  345.9 5.0 reshape.189
  350.9 3.2 copy.195
  354.2 4.8 reshape.188
  362.3 4.8 reshape.187
  367.1 3.3 fusion.48
  375.8 8.1 %copy.228 = bf16[3,768,768]{2,0,1:T(4,128)(2,1)} copy(bf16[3,768,768]{1,2,0:T(8,128)(2,1)} %pad_maximum_fusion) | data formatting | bytes 7077888
  384.0 4.9 copy.237
  389.6 12.2 %convolution_convert_fusion.1 = bf16[768,3072]{1,0:T(8,128)(2,1)} fusion(bf16[1152,3072]{1,0:T(8,128)(2,1)} %get-tuple-element.215, f32[1152,768]{1,0:T(8,128)} %copy-done.9, f32[768]{0:T(1024)S(1)} %copy-done.34, f32[1152]{0:T(1024)S(1)} %copy-done.25, f32[1152]{0:T(1024)S(1)} %broadcast_multiply_fusion.4, f32[768]{0:T(1024)S(1)} %copy-done.30), kind=kOutput, calls=%fused_computation.27 | convolution fusion | flops 5442600960 | bytes 15350784 | tf_op jit(solution)/shard_map/dot_general | solution.py:50
  401.9 11.1 %convolution_convert_fusion = bf16[768,3072]{1,0:T(8,128)(2,1)} fusion(bf16[1152,3072]{1,0:T(8,128)(2,1)} %get-tuple-element.203, f32[1152,768]{1,0:T(8,128)} %copy-done.13), kind=kOutput, calls=%fused_computation.26 | convolution fusion | flops 5439062016 | bytes 15335424 | tf_op jit(solution)/shard_map/dot_general | solution.py:50
  415.0 20.5 %reduce-scatter.25.cloned.1.call-done = bf16[96,2304]{1,0:T(8,128)(2,1)} async-done(((bf16[768,2304]{1,0:T(8,128)(2,1)}), bf16[96,2304]{1,0:T(8,128)(2,1)}) %reduce-scatter.25.cloned.1.call-update) | async-done | bytes 442384
  447.3 39.7 %psum.7 = f32[12,768]{1,0:T(8,128)S(1)} all-reduce(f32[12,768]{1,0:T(8,128)S(1)} %concatenate.3), channel_id=1, replica_groups=mesh['dp'=8,'mp'=4] {'dp','mp'}, use_global_device_ids=true, to_apply=%region_22.23 | all-reduce | flops 9216 | bytes 73728 | tf_op jit(solution)/shard_map/psum | solution.py:177
  495.2 4.6 convolution_add_fusion.5
  499.9 4.7 convolution_add_fusion.4
  504.6 46.3 %reduce-scatter.21.cloned.1.call-done = bf16[96,3072]{1,0:T(8,128)(2,1)} async-done(((bf16[768,3072]{1,0:T(8,128)(2,1)}), bf16[96,3072]{1,0:T(8,128)(2,1)}) %reduce-scatter.21.cloned.1.call-update) | async-done | bytes 589840 | tf_op jit(solution)/shard_map/reduce_scatter | solution.py:132
  550.9 5.8 convolution_add_fusion.3
  556.6 16.5 %reduce-scatter.27.cloned.1.call-done = bf16[192,96]{1,0:T(8,128)(2,1)} async-done(((bf16[768,96]{1,0:T(8,128)(2,1)}), bf16[192,96]{1,0:T(8,128)(2,1)}) %reduce-scatter.27.cloned.1.call-update) | async-done | bytes 36880
  577.1 18.5 %reduce-scatter.13.cloned.1.call-done = bf16[3,96,192]{1,2,0:T(8,128)(2,1)} async-done(((bf16[3,96,768]{1,2,0:T(8,128)(2,1)}), bf16[3,96,192]{1,2,0:T(8,128)(2,1)}) %reduce-scatter.13.cloned.1.call-update) | async-done | bytes 110608 | tf_op jit(solution)/shard_map/reduce_scatter | solution.py:133
  600.3 17.9 %reduce-scatter.19.cloned.1.call-done = bf16[96,768]{1,0:T(8,128)(2,1)} async-done(((bf16[96,3072]{1,0:T(8,128)(2,1)}), bf16[96,768]{1,0:T(8,128)(2,1)}) %reduce-scatter.19.cloned.1.call-update) | async-done | bytes 147472 | tf_op jit(solution)/shard_map/reduce_scatter | solution.py:133
  620.4 20.3 %reduce-scatter.23.cloned.1.call-done = bf16[96,768]{1,0:T(8,128)(2,1)} async-done(((bf16[96,3072]{1,0:T(8,128)(2,1)}), bf16[96,768]{1,0:T(8,128)(2,1)}) %reduce-scatter.23.cloned.1.call-update) | async-done | bytes 147472 | tf_op jit(solution)/shard_map/reduce_scatter | solution.py:133
  (197 shorter events, 76.3 us)
Async XLA Ops:
  7.2 40.9 %copy-start = (bf16[768,768]{1,0:T(8,128)(2,1)S(1)}, bf16[768,768]{1,0:T(8,128)(2,1)}, u32[]{:S(2)}) copy-start(bf16[768,768]{1,0:T(8,128)(2,1)} %param.37) | copy-start | bytes 3538948
  7.2 103.6 %all-gather.6.cloned.1.call-start = ((), (), s32[]{:S(2)}) async-start(), calls=%async_computation.8 | async-start | bytes 3981312 | tf_op jit(solution)/shard_map/all_gather | solution.py:69
  8.6 74.2 %copy-start.35 = (bf16[2,3,64]{2,0,1:T(2,128)(2,1)S(1)}, bf16[2,3,64]{2,0,1:T(2,128)(2,1)}, u32[]{:S(2)}) copy-start(bf16[2,3,64]{2,0,1:T(2,128)(2,1)} %param.35) | copy-start | bytes 2308
  30.3 65.6 %copy-start.31 = (bf16[6,768]{1,0:T(8,128)(2,1)S(1)}, bf16[6,768]{1,0:T(8,128)(2,1)}, u32[]{:S(2)}) copy-start(bf16[6,768]{1,0:T(8,128)(2,1)} %param.40) | copy-start | bytes 27652
  30.3 65.7 %copy-start.32 = (bf16[12,64]{1,0:T(8,128)(2,1)S(1)}, bf16[12,64]{1,0:T(8,128)(2,1)}, u32[]{:S(2)}) copy-start(bf16[12,64]{1,0:T(8,128)(2,1)} %param.38) | copy-start | bytes 4612
  30.3 78.9 %copy-start.6 = (bf16[4,288,768]{2,1,0:T(8,128)(2,1)S(1)}, bf16[4,288,768]{2,1,0:T(8,128)(2,1)}, u32[]{:S(2)}) copy-start(bf16[4,288,768]{2,1,0:T(8,128)(2,1)} %param.32) | copy-start | bytes 5308420
  32.6 161.1 %all-gather.8.cloned.1.call-start = ((), (), s32[]{:S(2)}) async-start(), calls=%async_computation.9 | async-start | bytes 1327104 | tf_op jit(solution)/shard_map/all_gather | solution.py:73
  48.0 152.2 %all-gather.10.cloned.1.call-start = ((), (), s32[]{:S(2)}) async-start(), calls=%async_computation.10 | async-start | bytes 5308416 | tf_op jit(solution)/shard_map/all_gather | solution.py:77
  65.6 148.4 %all-gather.12.cloned.1.call-start = ((), (), s32[]{:S(2)}) async-start(), calls=%async_computation.11 | async-start | bytes 5308416 | tf_op jit(solution)/shard_map/all_gather | solution.py:81
  82.7 330.3 %reduce-scatter.15.cloned.1.call-start = ((), (), s32[]{:S(2)}) async-start(), calls=%async_computation.13 | async-start | bytes 1327104 | tf_op jit(solution)/shard_map/reduce_scatter | solution.py:132
  95.9 118.1 %copy-start.33 = (f32[768]{0:T(1024)}, f32[768]{0:T(1024)S(1)}, u32[]{:S(2)}) copy-start(f32[768]{0:T(1024)S(1)} %get-tuple-element.161) | copy-start | bytes 9220
  96.0 162.7 %copy-start.29 = (f32[768]{0:T(1024)}, f32[768]{0:T(1024)S(1)}, u32[]{:S(2)}) copy-start(f32[768]{0:T(1024)S(1)} %get-tuple-element.163) | copy-start | bytes 9220
  120.5 21.9 %copy-start.3 = (bf16[4,288,12,64]{1,0,3,2:T(4,128)(2,1)}, bf16[4,288,12,64]{1,0,3,2:T(4,128)(2,1)S(1)}, u32[]{:S(2)}) copy-start(bf16[4,288,12,64]{1,0,3,2:T(4,128)(2,1)S(1)} %reshape.182) | copy-start | bytes 5308420
  154.3 25.5 %copy-start.15 = (bf16[4,288,12,64]{1,0,3,2:T(4,128)(2,1)S(1)}, bf16[4,288,12,64]{1,0,3,2:T(4,128)(2,1)}, u32[]{:S(2)}) copy-start(bf16[4,288,12,64]{1,0,3,2:T(4,128)(2,1)} %reshape.181) | copy-start | bytes 5308420
  197.8 1.8 copy-start.9
  200.2 58.4 %copy-start.24 = (f32[1152]{0:T(1024)}, f32[1152]{0:T(1024)S(1)}, u32[]{:S(2)}) copy-start(f32[1152]{0:T(1024)S(1)} %add_rsqrt_fusion.1) | copy-start | bytes 13828
  229.2 3.1 copy-start.36
  229.2 19.7 %slice-start = ((s8[4718592]{0:T(1024)(128)(4,1)}), s8[4194304]{0:T(1024)(128)(4,1)S(1)}, s32[]{:S(2)}) async-start(s8[4718592]{0:T(1024)(128)(4,1)} %bitcast.133), calls=%async_computation.20 | async-start | bytes 8388608
  232.3 16.7 %copy-start.13 = (f32[1152,768]{1,0:T(8,128)}, f32[1152,768]{1,0:T(8,128)S(1)}, u32[]{:S(2)}) copy-start(f32[1152,768]{1,0:T(8,128)S(1)} %get-tuple-element.184) | copy-start | bytes 10616836
  232.3 16.7 %copy-start.10 = (f32[1152,768]{1,0:T(8,128)S(1)}, f32[1152,768]{1,0:T(8,128)}, u32[]{:S(2)}) copy-start(f32[1152,768]{1,0:T(8,128)} %copy-done.9) | copy-start | bytes 10616836
  232.3 16.7 %slice-start.1 = ((s8[4718592]{0:T(1024)(128)(4,1)}), s8[524288]{0:T(1024)(128)(4,1)S(1)}, s32[]{:S(2)}) async-start(s8[4718592]{0:T(1024)(128)(4,1)} %bitcast.133), calls=%async_computation.21 | async-start | bytes 1048576
  258.7 3.6 copy-start.38
  260.5 1.8 copy-start.12
  310.9 18.6 %copy-start.5 = (bf16[4,288,12,64]{1,0,3,2:T(4,128)(2,1)S(1)}, bf16[4,288,12,64]{1,0,3,2:T(4,128)(2,1)}, u32[]{:S(2)}) copy-start(bf16[4,288,12,64]{1,0,3,2:T(4,128)(2,1)} %reshape.183) | copy-start | bytes 5308420
  325.6 4.0 copy-start.2
  329.6 3.7 copy-start.4
  333.2 102.3 %reduce-scatter.25.cloned.1.call-start = ((), (), s32[]{:S(2)}) async-start(), calls=%async_computation.18 | async-start | bytes 3981312
  333.3 9.4 %copy-start.14 = (bf16[4,288,12,64]{1,3,2,0:T(8,128)(2,1)S(1)}, bf16[4,288,12,64]{1,3,2,0:T(8,128)(2,1)}, u32[]{:S(2)}) copy-start(bf16[4,288,12,64]{1,3,2,0:T(8,128)(2,1)} %get-tuple-element.213) | copy-start | bytes 5308420
  342.7 8.3 %copy-start.8 = (bf16[4,288,12,64]{1,3,2,0:T(8,128)(2,1)S(1)}, bf16[4,288,12,64]{1,3,2,0:T(8,128)(2,1)}, u32[]{:S(2)}) copy-start(bf16[4,288,12,64]{1,3,2,0:T(8,128)(2,1)} %fusion.31) | copy-start | bytes 5308420
  354.2 4.8 copy-start.11
  362.3 4.8 copy-start.16
  367.1 3.3 copy-start.17
  367.1 3.4 copy-start.37
  388.9 104.6 %reduce-scatter.17.cloned.1.call-start = ((), (), s32[]{:S(2)}) async-start(), calls=%async_computation.14 | async-start | bytes 5308416 | tf_op jit(solution)/shard_map/reduce_scatter | solution.py:132
  401.8 149.0 %reduce-scatter.21.cloned.1.call-start = ((), (), s32[]{:S(2)}) async-start(), calls=%async_computation.16 | async-start | bytes 5308416 | tf_op jit(solution)/shard_map/reduce_scatter | solution.py:132
  413.0 25.4 %copy-start.26 = (f32[768]{0:T(1024)S(1)}, f32[768]{0:T(1024)}, u32[]{:S(2)}) copy-start(f32[768]{0:T(1024)} %get-tuple-element.156) | copy-start | bytes 9220
  413.0 25.5 %copy-start.20 = (f32[3,96,192]{2,1,0:T(8,128)S(1)}, f32[3,96,192]{2,1,0:T(8,128)}, u32[]{:S(2)}) copy-start(f32[3,96,192]{2,1,0:T(8,128)} %param.42) | copy-start | bytes 663556
  413.0 25.6 %copy-start.21 = (f32[3,96,192]{2,1,0:T(8,128)S(1)}, f32[3,96,192]{2,1,0:T(8,128)}, u32[]{:S(2)}) copy-start(f32[3,96,192]{2,1,0:T(8,128)} %param.43) | copy-start | bytes 663556
  413.0 31.4 %copy-start.28 = (f32[768]{0:T(1024)S(1)}, f32[768]{0:T(1024)}, u32[]{:S(2)}) copy-start(f32[768]{0:T(1024)} %get-tuple-element.185) | copy-start | bytes 9220
  413.0 33.5 %copy-start.27 = (f32[768]{0:T(1024)S(1)}, f32[768]{0:T(1024)}, u32[]{:S(2)}) copy-start(f32[768]{0:T(1024)} %get-tuple-element.183) | copy-start | bytes 9220
  413.0 160.1 %reduce-scatter.27.cloned.1.call-start = ((), (), s32[]{:S(2)}) async-start(), calls=%async_computation.19 | async-start | bytes 245760
  414.9 180.6 %reduce-scatter.13.cloned.1.call-start = ((), (), s32[]{:S(2)}) async-start(), calls=%async_computation.12 | async-start | bytes 737280 | tf_op jit(solution)/shard_map/reduce_scatter | solution.py:133
  438.3 179.8 %reduce-scatter.19.cloned.1.call-start = ((), (), s32[]{:S(2)}) async-start(), calls=%async_computation.15 | async-start | bytes 737280 | tf_op jit(solution)/shard_map/reduce_scatter | solution.py:133
  493.5 147.2 %reduce-scatter.23.cloned.1.call-start = ((), (), s32[]{:S(2)}) async-start(), calls=%async_computation.17 | async-start | bytes 737280 | tf_op jit(solution)/shard_map/reduce_scatter | solution.py:133
  495.2 4.7 copy-start.18
  556.6 61.6 %copy-start.22 = (f32[96,768]{1,0:T(8,128)S(1)}, f32[96,768]{1,0:T(8,128)}, u32[]{:S(2)}) copy-start(f32[96,768]{1,0:T(8,128)} %param.50) | copy-start | bytes 884740
  556.6 61.6 %copy-start.23 = (f32[96,768]{1,0:T(8,128)S(1)}, f32[96,768]{1,0:T(8,128)}, u32[]{:S(2)}) copy-start(f32[96,768]{1,0:T(8,128)} %param.51) | copy-start | bytes 884740
  595.5 47.6 %copy-start.1 = (bf16[768,768]{1,0:T(8,128)(2,1)S(1)}, bf16[768,768]{1,0:T(8,128)(2,1)}, u32[]{:S(2)}) copy-start(bf16[768,768]{1,0:T(8,128)(2,1)} %param.37) | copy-start | bytes 3538948
  (5 other events, 5.3 us)
Sparse Core Ops, SparseCore 0:
  32.7 33.7 all-gather.5
  68.9 24.0 all-gather.7
  94.9 38.9 all-gather.9
  135.6 38.9 all-gather.11
  333.3 35.0 reduce-scatter.14
  389.0 46.4 reduce-scatter.24
  439.3 54.1 reduce-scatter.16
  496.9 53.8 reduce-scatter.20
  553.8 19.3 reduce-scatter.26
  575.3 20.2 reduce-scatter.12
  597.8 20.2 reduce-scatter.18
  620.3 20.3 reduce-scatter.22
where the time goes:
time: 657 us; the launch traced here: 650 us
  matrix products  189 us (29%)
  waiting for transfers between devices  142 us (22%)
  blocking collectives  133 us (20%)
  local copies, waits for them, and re-layouts  109 us (17%)
  other arithmetic  61.6 us (9%)
  between operations  15.1 us (2%)
    dot_general x18, matrix products, mm(): lax.dot_general(a, b, (dims, ((), ())), preferred_element_type=jnp.float32)  124 us
    reduce_scatter x3, waiting for transfers between devices, reduce_grad(): lax.psum_scatter(part, 'mp', scatter_dimension=part.ndim - 1, tiled=True)  56.6 us
    reduce_scatter x3, waiting for transfers between devices, reduce_grad(): lax.psum_scatter(part, 'dp', scatter_dimension=part.ndim - 2, tiled=True)  47.9 us
    unnamed x109, local copies, waits for them, and re-layouts  41.8 us
    psum x1, blocking collectives, per_device(): lax.psum(jnp.concatenate([vector_grad, total(dexpanded).reshape(4, D)]),...  39.7 us
    unnamed x14, waiting for transfers between devices  37.2 us
    reshape x5, local copies, waits for them, and re-layouts, split(): return t.reshape(rows, length, heads, HEAD)  26.8 us
    sub x1, other arithmetic, per_device(): weights = jnp.exp(scores - row_max)  25.5 us
  transfers between devices with their start and end apart: 12, of which 7 were waited for; matrix products, arithmetic and copies ran while one was open for 36% of the time, Pallas kernels for 0%

commit v1 on v0

--- a/solution.py
+++ b/solution.py
@@ -175,7 +175,7 @@
         ]
     )
     vector_grad = lax.psum(
-        jnp.concatenate([vector_grad, total(dexpanded).reshape(4, D)]), ("dp", "mp")
+        lax.psum(jnp.concatenate([vector_grad, total(dexpanded).reshape(4, D)]), "dp"), "mp"
     )
     dp, mp = (lax.axis_index("dp"), lax.axis_index("mp"))
     groups, parts = (lax.axis_size("mp"), lax.axis_size("dp"))

time: 657 us -> 657 us (level)
    psum x0 -> x1, blocking collectives: none -> 19.4 us  [per_device(): lax.psum(lax.psum(jnp.concatenate([vector_grad, total(dexpanded).reshape(...]
    psum x1, blocking collectives: 39.7 us -> 24 us  [per_device(): lax.psum(jnp.concatenate([vector_grad, total(dexpanded).reshape(4, D)]),...]
  transfers between devices with their start and end apart: 12 -> 12, of which waited for: 7 -> 6; matrix products, arithmetic and copies ran while one was open for 36% -> 36% of each run, Pallas kernels for 0% -> 0%
where the time goes in v1:
time: 657 us; the launch traced here: 650 us
  matrix products  189 us (29%)
  waiting for transfers between devices  138 us (21%)
  blocking collectives  137 us (21%)
  local copies, waits for them, and re-layouts  109 us (17%)
  other arithmetic  61.6 us (9%)
  between operations  15.1 us (2%)
    dot_general x18, matrix products, mm(): lax.dot_general(a, b, (dims, ((), ())), preferred_element_type=jnp.float32)  124 us
    reduce_scatter x3, waiting for transfers between devices, reduce_grad(): lax.psum_scatter(part, 'mp', scatter_dimension=part.ndim - 1, tiled=True)  56.6 us
    reduce_scatter x3, waiting for transfers between devices, reduce_grad(): lax.psum_scatter(part, 'dp', scatter_dimension=part.ndim - 2, tiled=True)  44.3 us
    unnamed x109, local copies, waits for them, and re-layouts  41.8 us
    unnamed x14, waiting for transfers between devices  37.2 us
    reshape x5, local copies, waits for them, and re-layouts, split(): return t.reshape(rows, length, heads, HEAD)  26.8 us
    sub x1, other arithmetic, per_device(): weights = jnp.exp(scores - row_max)  25.5 us
    psum x1, blocking collectives, per_device(): lax.psum(jnp.concatenate([vector_grad, total(dexpanded).reshape(4, D)]),...  24 us
  transfers between devices with their start and end apart: 12, of which 6 were waited for; matrix products, arithmetic and copies ran while one was open for 36% of the time, Pallas kernels for 0%

profile of v1, /device:TPU:0, one launch (start us, length us, event | category | flops | bytes accessed | tf_op | source)
XLA Modules:
  0.0 650.1 jit_solution(9815383279570289068)
XLA Ops:
  8.6 21.7 %all_gather.30 = bf16[3,96,768]{1,0,2:T(4,128)(2,1)} all-gather(bf16[3,96,192]{1,0,2:T(4,128)(2,1)S(1)} %copy.234), channel_id=1, replica_groups=mesh['dp'=8,'mp'=4] {'mp'}, dimensions={2}, use_global_device_ids=true | all-gather | bytes 552960 | tf_op jit(solution)/shard_map/all_gather | solution.py:70
  33.6 13.6 %all_gather.33 = bf16[768,96]{1,0:T(8,128)(2,1)S(1)} all-gather(bf16[192,96]{1,0:T(8,128)(2,1)S(1)} %constant_dynamic-slice_fusion.2), channel_id=1, replica_groups=mesh['dp'=8,'mp'=4] {'mp'}, dimensions={0}, use_global_device_ids=true | all-gather | bytes 184320 | tf_op jit(solution)/shard_map/all_gather | solution.py:74
  48.1 17.4 %all_gather.35 = bf16[96,3072]{1,0:T(8,128)(2,1)} all-gather(bf16[96,768]{1,0:T(8,128)(2,1)S(1)} %constant_dynamic-slice_fusion.1), channel_id=1, replica_groups=mesh['dp'=8,'mp'=4] {'mp'}, dimensions={1}, use_global_device_ids=true | all-gather | bytes 737280 | tf_op jit(solution)/shard_map/all_gather | solution.py:78
  66.9 15.8 %all_gather.38 = bf16[3072,96]{0,1:T(8,128)(2,1)} all-gather(bf16[768,96]{0,1:T(8,128)(2,1)S(1)} %copy.235), channel_id=1, replica_groups=mesh['dp'=8,'mp'=4] {'mp'}, dimensions={0}, use_global_device_ids=true | all-gather | bytes 737280 | tf_op jit(solution)/shard_map/all_gather | solution.py:82
  82.8 11.9 %all_gather.32 = bf16[2,12,64]{2,0,1:T(2,128)(2,1)S(1)} all-gather(bf16[2,3,64]{2,0,1:T(2,128)(2,1)S(1)} %copy-done.35), channel_id=1, replica_groups=mesh['dp'=8,'mp'=4] {'mp'}, dimensions={1}, use_global_device_ids=true | all-gather | bytes 3840 | tf_op jit(solution)/shard_map/all_gather | solution.py:85
  96.0 13.1 %all-gather = bf16[4,12,64]{2,1,0:T(8,128)(2,1)S(1)} all-gather(bf16[1,12,64]{2,1,0:T(8,128)(2,1)S(1)} %bitcast.132), channel_id=1, replica_groups=mesh['dp'=8,'mp'=4] {'mp'}, dimensions={0}, use_global_device_ids=true | all-gather | bytes 7680 | tf_op jit(solution)/shard_map/all_gather | solution.py:88
  110.8 4.9 fusion.27
  115.7 4.8 reshape.182
  120.5 5.6 fusion.29
  126.1 5.7 reshape.183
  131.8 5.0 fusion.28
  136.8 5.6 reshape.181
  142.4 11.9 %fusion.36 = f32[4,12,288,288]{2,3,1,0:T(8,128)} fusion(bf16[4,288,12,64]{1,0,3,2:T(4,128)(2,1)} %reshape.183, bf16[4,288,12,64]{1,0,3,2:T(4,128)(2,1)S(1)} %reshape.182), kind=kOutput, calls=%fused_computation.80 | convolution fusion | flops 509607936 | bytes 19464192 | tf_op jit(solution)/shard_map/rqhc,rkhc->rhqk/dot_general | solution.py:104
  154.3 25.5 %fusion.85 = (f32[4,12,288]{2,1,0:T(8,128)S(1)}, f32[4,12,288,288]{2,3,1,0:T(8,128)}) fusion(f32[4,12,288,288]{2,3,1,0:T(8,128)} %fusion.36, pred[4,288,288]{1,2,0:T(8,128)(4,1)S(1)} %broadcast_compare_fusion), kind=kOutput, calls=%fused_computation.169 | output fusion | flops 23888160 | bytes 32237568 | tf_op jit(solution)/shard_map/sub | solution.py:109
  179.8 9.3 %convert_bitcast_fusion.1 = bf16[4,288,12,64]{1,3,2,0:T(8,128)(2,1)S(1)} fusion(bf16[4,288,12,64]{1,0,3,2:T(4,128)(2,1)S(1)} %copy-done.15, f32[4,12,288,288]{2,3,1,0:T(8,128)} %get-tuple-element.200, f32[4,12,288]{2,1,0:T(8,128)S(1)} %get-tuple-element.199), kind=kOutput, calls=%fused_computation.75 | convolution fusion | flops 518455296 | bytes 19519488 | tf_op jit(solution)/shard_map/rhqk,rkhc->rqhc/dot_general | solution.py:112
  193.6 4.2 fusion.86
  200.3 13.7 %multiply_convert_fusion.1 = (bf16[1152,3072]{1,0:T(8,128)(2,1)}, f32[1152,3072]{1,0:T(8,128)}) fusion(f32[3072]{0:T(1024)S(1)} %reshape.194, bf16[768,3072]{1,0:T(8,128)(2,1)} %all-gather.10.cloned.1.call-done, f32[1152,768]{1,0:T(8,128)} %copy-done.9, f32[768]{0:T(1024)S(1)} %get-tuple-element.161, f32[1152]{0:T(1024)S(1)} %add_rsqrt_fusion.1, ...), kind=kOutput, calls=%fused_computation.14 | convolution fusion | flops 5461475328 | bytes 29518848 | tf_op jit(solution)/shard_map/dot_general | solution.py:50
  214.0 11.8 %fusion.87 = (f32[1152]{0:T(1024)S(1)}, f32[1152,768]{1,0:T(8,128)S(1)}) fusion(f32[768]{0:T(1024)S(1)} %get-tuple-element.160, bf16[1152,3072]{1,0:T(8,128)(2,1)} %get-tuple-element.203, bf16[3072,768]{0,1:T(8,128)(2,1)} %all-gather.12.cloned.1.call-done, f32[768]{0:T(1024)S(1)} %get-tuple-element.161, f32[1152]{0:T(1024)S(1)} %add_rsqrt_fusion.1, ...), kind=kOutput, calls=%fused_computation.171 | convolution fusion | flops 5442010112 | bytes 18897408 | tf_op jit(solution)/shard_map/dot_general | solution.py:50
  232.3 16.6 %convert_reduce_fusion = (f32[3072]{0:T(1024)}, bf16[1152,3072]{1,0:T(8,128)(2,1)}) fusion(f32[1152,3072]{1,0:T(8,128)} %get-tuple-element.204, bf16[3072,768]{0,1:T(8,128)(2,1)S(1)} %copy-done.36, f32[1152,768]{1,0:T(8,128)S(1)} %get-tuple-element.184), kind=kOutput, calls=%fused_computation.13 | convolution fusion | flops 5486244864 | bytes 29503488 | tf_op jit(solution)/shard_map/dot_general | solution.py:50
  249.0 9.7 %multiply_reduce_fusion.1 = (f32[768]{0:T(1024)}, f32[1152]{0:T(1024)S(1)}, f32[1152]{0:T(1024)S(1)}, f32[768]{0:T(1024)}, f32[1152,768]{1,0:T(8,128)S(1)}) fusion(f32[1152,768]{1,0:T(8,128)S(1)} %copy-done.10, f32[1152]{0:T(1024)S(1)} %add_rsqrt_fusion.1, f32[1152]{0:T(1024)S(1)} %broadcast_multiply_fusion.4, f32[768]{0:T(1024)S(1)} %get-tuple-element.163, ...), kind=kOutput, calls=%fused_computation.54 | convolution fusion | flops 5444661248 | bytes 22440960 | tf_op jit(solution)/shard_map/dot_general | solution.py:50
  263.8 4.7 reshape.204
  268.5 6.1 copy.188
  274.6 12.8 %convert_reduce_fusion.1 = (f32[12,64]{1,0:T(8,128)}, bf16[4,288,12,64]{1,3,2,0:T(8,128)(2,1)}) fusion(bf16[4,288,12,64]{1,3,2,0:T(8,128)(2,1)S(1)} %copy.188, f32[4,12,288,288]{2,3,1,0:T(8,128)} %get-tuple-element.200, f32[4,12,288]{2,1,0:T(8,128)S(1)} %get-tuple-element.199), kind=kOutput, calls=%fused_computation.28 | convolution fusion | flops 520224000 | bytes 19522560 | tf_op jit(solution)/shard_map/rhqk,rqhc->rkhc/dot_general | solution.py:146
  287.4 18.2 %multiply_reduce_fusion = (f32[4,12,288]{2,1,0:T(8,128)S(1)}, f32[4,12,288,288]{2,3,1,0:T(8,128)}) fusion(f32[4,12,288,288]{2,3,1,0:T(8,128)} %get-tuple-element.200, f32[4,12,288]{2,1,0:T(8,128)S(1)} %get-tuple-element.199, bf16[4,288,12,64]{1,3,2,0:T(8,128)(2,1)S(1)} %copy.188, bf16[4,288,12,64]{1,0,3,2:T(4,128)(2,1)} %reshape.181), kind=kOutput, calls=%fused_computation.2 | convolution fusion | flops 521538048 | bytes 35500032 | tf_op jit(solution)/shard_map/rqhc,rkhc->rhqk/dot_general | solution.py:147
  305.6 5.3 convolution_convert_fusion.4
  310.9 14.6 %multiply_convert_fusion = bf16[4,12,288,288]{2,3,1,0:T(8,128)(2,1)S(1)} fusion(f32[4,12,288,288]{2,3,1,0:T(8,128)} %get-tuple-element.209, f32[4,12,288]{2,1,0:T(8,128)S(1)} %get-tuple-element.208, f32[4,12,288,288]{2,3,1,0:T(8,128)} %get-tuple-element.200, f32[4,12,288]{2,1,0:T(8,128)S(1)} %get-tuple-element.199), kind=kLoop, calls=%fused_computation.1 | loop fusion | flops 15925248 | bytes 39923712 | tf_op jit(solution)/shard_map/convert_element_type | solution.py:149
  325.6 4.0 copy-done.2
  329.6 3.6 convert_reduce_fusion.2
  333.3 9.4 %fusion.31 = bf16[4,288,12,64]{1,3,2,0:T(8,128)(2,1)} fusion(bf16[4,12,288,288]{2,3,1,0:T(8,128)(2,1)} %copy-done.2, bf16[4,288,12,64]{1,0,3,2:T(4,128)(2,1)S(1)} %copy-done.4), kind=kOutput, calls=%fused_computation.73 | convolution fusion | flops 511377408 | bytes 11501568 | tf_op jit(solution)/shard_map/rhqk,rqhc->rkhc/dot_general | solution.py:153
  345.9 5.0 reshape.189
  354.2 4.8 reshape.188
  362.3 4.8 reshape.187
  367.1 3.3 fusion.48
  375.8 8.1 %copy.228 = bf16[3,768,768]{2,0,1:T(4,128)(2,1)} copy(bf16[3,768,768]{1,2,0:T(8,128)(2,1)} %pad_maximum_fusion) | data formatting | bytes 7077888
  384.0 4.9 copy.237
  389.6 12.2 %convolution_convert_fusion.1 = bf16[768,3072]{1,0:T(8,128)(2,1)} fusion(bf16[1152,3072]{1,0:T(8,128)(2,1)} %get-tuple-element.215, f32[1152,768]{1,0:T(8,128)} %copy-done.9, f32[768]{0:T(1024)S(1)} %copy-done.34, f32[1152]{0:T(1024)S(1)} %copy-done.25, f32[1152]{0:T(1024)S(1)} %broadcast_multiply_fusion.4, f32[768]{0:T(1024)S(1)} %copy-done.30), kind=kOutput, calls=%fused_computation.27 | convolution fusion | flops 5442600960 | bytes 15350784 | tf_op jit(solution)/shard_map/dot_general | solution.py:50
  401.9 11.1 %convolution_convert_fusion = bf16[768,3072]{1,0:T(8,128)(2,1)} fusion(bf16[1152,3072]{1,0:T(8,128)(2,1)} %get-tuple-element.203, f32[1152,768]{1,0:T(8,128)} %copy-done.13), kind=kOutput, calls=%fused_computation.26 | convolution fusion | flops 5439062016 | bytes 15335424 | tf_op jit(solution)/shard_map/dot_general | solution.py:50
  415.0 20.5 %reduce-scatter.25.cloned.1.call-done = bf16[96,2304]{1,0:T(8,128)(2,1)} async-done(((bf16[768,2304]{1,0:T(8,128)(2,1)}), bf16[96,2304]{1,0:T(8,128)(2,1)}) %reduce-scatter.25.cloned.1.call-update) | async-done | bytes 442384
  447.3 24.0 %psum.14 = f32[12,768]{1,0:T(8,128)S(1)} all-reduce(f32[12,768]{1,0:T(8,128)S(1)} %concatenate.3), channel_id=1, replica_groups=mesh['dp'=8,'mp'=4] {'dp'}, use_global_device_ids=true, to_apply=%region_22.23 | all-reduce | flops 9216 | bytes 73728 | tf_op jit(solution)/shard_map/psum | solution.py:178
  471.3 19.4 %psum.15 = f32[12,768]{1,0:T(8,128)S(1)} all-reduce(f32[12,768]{1,0:T(8,128)S(1)} %psum.14), channel_id=1, replica_groups=mesh['dp'=8,'mp'=4] {'mp'}, use_global_device_ids=true, to_apply=%region_23.24 | all-reduce | flops 9216 | bytes 73728 | tf_op jit(solution)/shard_map/psum | solution.py:177
  497.1 4.6 convolution_add_fusion.5
  501.8 4.8 convolution_add_fusion.4
  506.6 44.2 %reduce-scatter.21.cloned.1.call-done = bf16[96,3072]{1,0:T(8,128)(2,1)} async-done(((bf16[768,3072]{1,0:T(8,128)(2,1)}), bf16[96,3072]{1,0:T(8,128)(2,1)}) %reduce-scatter.21.cloned.1.call-update) | async-done | bytes 589840 | tf_op jit(solution)/shard_map/reduce_scatter | solution.py:132
  550.9 5.8 convolution_add_fusion.3
  556.6 16.5 %reduce-scatter.27.cloned.1.call-done = bf16[192,96]{1,0:T(8,128)(2,1)} async-done(((bf16[768,96]{1,0:T(8,128)(2,1)}), bf16[192,96]{1,0:T(8,128)(2,1)}) %reduce-scatter.27.cloned.1.call-update) | async-done | bytes 36880
  577.1 18.5 %reduce-scatter.13.cloned.1.call-done = bf16[3,96,192]{1,2,0:T(8,128)(2,1)} async-done(((bf16[3,96,768]{1,2,0:T(8,128)(2,1)}), bf16[3,96,192]{1,2,0:T(8,128)(2,1)}) %reduce-scatter.13.cloned.1.call-update) | async-done | bytes 110608 | tf_op jit(solution)/shard_map/reduce_scatter | solution.py:133
  600.3 17.9 %reduce-scatter.19.cloned.1.call-done = bf16[96,768]{1,0:T(8,128)(2,1)} async-done(((bf16[96,3072]{1,0:T(8,128)(2,1)}), bf16[96,768]{1,0:T(8,128)(2,1)}) %reduce-scatter.19.cloned.1.call-update) | async-done | bytes 147472 | tf_op jit(solution)/shard_map/reduce_scatter | solution.py:133
  620.4 20.2 %reduce-scatter.23.cloned.1.call-done = bf16[96,768]{1,0:T(8,128)(2,1)} async-done(((bf16[96,3072]{1,0:T(8,128)(2,1)}), bf16[96,768]{1,0:T(8,128)(2,1)}) %reduce-scatter.23.cloned.1.call-update) | async-done | bytes 147472 | tf_op jit(solution)/shard_map/reduce_scatter | solution.py:133
  (198 shorter events, 77.9 us)
Async XLA Ops:
  7.2 40.9 %copy-start = (bf16[768,768]{1,0:T(8,128)(2,1)S(1)}, bf16[768,768]{1,0:T(8,128)(2,1)}, u32[]{:S(2)}) copy-start(bf16[768,768]{1,0:T(8,128)(2,1)} %param.37) | copy-start | bytes 3538948
  7.2 103.6 %all-gather.6.cloned.1.call-start = ((), (), s32[]{:S(2)}) async-start(), calls=%async_computation.8 | async-start | bytes 3981312 | tf_op jit(solution)/shard_map/all_gather | solution.py:69
  8.6 74.2 %copy-start.35 = (bf16[2,3,64]{2,0,1:T(2,128)(2,1)S(1)}, bf16[2,3,64]{2,0,1:T(2,128)(2,1)}, u32[]{:S(2)}) copy-start(bf16[2,3,64]{2,0,1:T(2,128)(2,1)} %param.35) | copy-start | bytes 2308
  30.3 65.6 %copy-start.31 = (bf16[6,768]{1,0:T(8,128)(2,1)S(1)}, bf16[6,768]{1,0:T(8,128)(2,1)}, u32[]{:S(2)}) copy-start(bf16[6,768]{1,0:T(8,128)(2,1)} %param.40) | copy-start | bytes 27652
  30.3 65.7 %copy-start.32 = (bf16[12,64]{1,0:T(8,128)(2,1)S(1)}, bf16[12,64]{1,0:T(8,128)(2,1)}, u32[]{:S(2)}) copy-start(bf16[12,64]{1,0:T(8,128)(2,1)} %param.38) | copy-start | bytes 4612
  30.3 78.9 %copy-start.6 = (bf16[4,288,768]{2,1,0:T(8,128)(2,1)S(1)}, bf16[4,288,768]{2,1,0:T(8,128)(2,1)}, u32[]{:S(2)}) copy-start(bf16[4,288,768]{2,1,0:T(8,128)(2,1)} %param.32) | copy-start | bytes 5308420
  32.6 161.1 %all-gather.8.cloned.1.call-start = ((), (), s32[]{:S(2)}) async-start(), calls=%async_computation.9 | async-start | bytes 1327104 | tf_op jit(solution)/shard_map/all_gather | solution.py:73
  48.0 152.2 %all-gather.10.cloned.1.call-start = ((), (), s32[]{:S(2)}) async-start(), calls=%async_computation.10 | async-start | bytes 5308416 | tf_op jit(solution)/shard_map/all_gather | solution.py:77
  65.6 148.4 %all-gather.12.cloned.1.call-start = ((), (), s32[]{:S(2)}) async-start(), calls=%async_computation.11 | async-start | bytes 5308416 | tf_op jit(solution)/shard_map/all_gather | solution.py:81
  82.7 330.3 %reduce-scatter.15.cloned.1.call-start = ((), (), s32[]{:S(2)}) async-start(), calls=%async_computation.13 | async-start | bytes 1327104 | tf_op jit(solution)/shard_map/reduce_scatter | solution.py:132
  95.9 118.1 %copy-start.33 = (f32[768]{0:T(1024)}, f32[768]{0:T(1024)S(1)}, u32[]{:S(2)}) copy-start(f32[768]{0:T(1024)S(1)} %get-tuple-element.161) | copy-start | bytes 9220
  96.0 162.7 %copy-start.29 = (f32[768]{0:T(1024)}, f32[768]{0:T(1024)S(1)}, u32[]{:S(2)}) copy-start(f32[768]{0:T(1024)S(1)} %get-tuple-element.163) | copy-start | bytes 9220
  120.5 21.9 %copy-start.3 = (bf16[4,288,12,64]{1,0,3,2:T(4,128)(2,1)}, bf16[4,288,12,64]{1,0,3,2:T(4,128)(2,1)S(1)}, u32[]{:S(2)}) copy-start(bf16[4,288,12,64]{1,0,3,2:T(4,128)(2,1)S(1)} %reshape.182) | copy-start | bytes 5308420
  154.3 25.5 %copy-start.15 = (bf16[4,288,12,64]{1,0,3,2:T(4,128)(2,1)S(1)}, bf16[4,288,12,64]{1,0,3,2:T(4,128)(2,1)}, u32[]{:S(2)}) copy-start(bf16[4,288,12,64]{1,0,3,2:T(4,128)(2,1)} %reshape.181) | copy-start | bytes 5308420
  197.8 1.8 copy-start.9
  200.2 58.4 %copy-start.24 = (f32[1152]{0:T(1024)}, f32[1152]{0:T(1024)S(1)}, u32[]{:S(2)}) copy-start(f32[1152]{0:T(1024)S(1)} %add_rsqrt_fusion.1) | copy-start | bytes 13828
  229.2 3.1 copy-start.36
  229.2 19.7 %slice-start = ((s8[4718592]{0:T(1024)(128)(4,1)}), s8[4194304]{0:T(1024)(128)(4,1)S(1)}, s32[]{:S(2)}) async-start(s8[4718592]{0:T(1024)(128)(4,1)} %bitcast.133), calls=%async_computation.20 | async-start | bytes 8388608
  232.3 16.7 %copy-start.13 = (f32[1152,768]{1,0:T(8,128)}, f32[1152,768]{1,0:T(8,128)S(1)}, u32[]{:S(2)}) copy-start(f32[1152,768]{1,0:T(8,128)S(1)} %get-tuple-element.184) | copy-start | bytes 10616836
  232.3 16.7 %copy-start.10 = (f32[1152,768]{1,0:T(8,128)S(1)}, f32[1152,768]{1,0:T(8,128)}, u32[]{:S(2)}) copy-start(f32[1152,768]{1,0:T(8,128)} %copy-done.9) | copy-start | bytes 10616836
  232.3 16.7 %slice-start.1 = ((s8[4718592]{0:T(1024)(128)(4,1)}), s8[524288]{0:T(1024)(128)(4,1)S(1)}, s32[]{:S(2)}) async-start(s8[4718592]{0:T(1024)(128)(4,1)} %bitcast.133), calls=%async_computation.21 | async-start | bytes 1048576
  258.7 3.6 copy-start.38
  260.5 1.8 copy-start.12
  310.9 18.6 %copy-start.5 = (bf16[4,288,12,64]{1,0,3,2:T(4,128)(2,1)S(1)}, bf16[4,288,12,64]{1,0,3,2:T(4,128)(2,1)}, u32[]{:S(2)}) copy-start(bf16[4,288,12,64]{1,0,3,2:T(4,128)(2,1)} %reshape.183) | copy-start | bytes 5308420
  325.6 4.0 copy-start.2
  329.6 3.7 copy-start.4
  333.2 102.3 %reduce-scatter.25.cloned.1.call-start = ((), (), s32[]{:S(2)}) async-start(), calls=%async_computation.18 | async-start | bytes 3981312
  333.3 9.4 %copy-start.14 = (bf16[4,288,12,64]{1,3,2,0:T(8,128)(2,1)S(1)}, bf16[4,288,12,64]{1,3,2,0:T(8,128)(2,1)}, u32[]{:S(2)}) copy-start(bf16[4,288,12,64]{1,3,2,0:T(8,128)(2,1)} %get-tuple-element.213) | copy-start | bytes 5308420
  342.7 8.3 %copy-start.8 = (bf16[4,288,12,64]{1,3,2,0:T(8,128)(2,1)S(1)}, bf16[4,288,12,64]{1,3,2,0:T(8,128)(2,1)}, u32[]{:S(2)}) copy-start(bf16[4,288,12,64]{1,3,2,0:T(8,128)(2,1)} %fusion.31) | copy-start | bytes 5308420
  354.2 4.8 copy-start.11
  362.3 4.8 copy-start.16
  367.1 3.3 copy-start.17
  367.1 3.4 copy-start.37
  388.9 106.5 %reduce-scatter.17.cloned.1.call-start = ((), (), s32[]{:S(2)}) async-start(), calls=%async_computation.14 | async-start | bytes 5308416 | tf_op jit(solution)/shard_map/reduce_scatter | solution.py:132
  401.8 149.0 %reduce-scatter.21.cloned.1.call-start = ((), (), s32[]{:S(2)}) async-start(), calls=%async_computation.16 | async-start | bytes 5308416 | tf_op jit(solution)/shard_map/reduce_scatter | solution.py:132
  413.0 25.4 %copy-start.26 = (f32[768]{0:T(1024)S(1)}, f32[768]{0:T(1024)}, u32[]{:S(2)}) copy-start(f32[768]{0:T(1024)} %get-tuple-element.156) | copy-start | bytes 9220
  413.0 25.5 %copy-start.20 = (f32[3,96,192]{2,1,0:T(8,128)S(1)}, f32[3,96,192]{2,1,0:T(8,128)}, u32[]{:S(2)}) copy-start(f32[3,96,192]{2,1,0:T(8,128)} %param.42) | copy-start | bytes 663556
  413.0 25.6 %copy-start.21 = (f32[3,96,192]{2,1,0:T(8,128)S(1)}, f32[3,96,192]{2,1,0:T(8,128)}, u32[]{:S(2)}) copy-start(f32[3,96,192]{2,1,0:T(8,128)} %param.43) | copy-start | bytes 663556
  413.0 31.4 %copy-start.28 = (f32[768]{0:T(1024)S(1)}, f32[768]{0:T(1024)}, u32[]{:S(2)}) copy-start(f32[768]{0:T(1024)} %get-tuple-element.185) | copy-start | bytes 9220
  413.0 33.5 %copy-start.27 = (f32[768]{0:T(1024)S(1)}, f32[768]{0:T(1024)}, u32[]{:S(2)}) copy-start(f32[768]{0:T(1024)} %get-tuple-element.183) | copy-start | bytes 9220
  413.0 160.1 %reduce-scatter.27.cloned.1.call-start = ((), (), s32[]{:S(2)}) async-start(), calls=%async_computation.19 | async-start | bytes 245760
  414.9 180.6 %reduce-scatter.13.cloned.1.call-start = ((), (), s32[]{:S(2)}) async-start(), calls=%async_computation.12 | async-start | bytes 737280 | tf_op jit(solution)/shard_map/reduce_scatter | solution.py:133
  438.3 179.8 %reduce-scatter.19.cloned.1.call-start = ((), (), s32[]{:S(2)}) async-start(), calls=%async_computation.15 | async-start | bytes 737280 | tf_op jit(solution)/shard_map/reduce_scatter | solution.py:133
  495.5 145.2 %reduce-scatter.23.cloned.1.call-start = ((), (), s32[]{:S(2)}) async-start(), calls=%async_computation.17 | async-start | bytes 737280 | tf_op jit(solution)/shard_map/reduce_scatter | solution.py:133
  497.1 4.6 copy-start.18
  556.6 61.6 %copy-start.22 = (f32[96,768]{1,0:T(8,128)S(1)}, f32[96,768]{1,0:T(8,128)}, u32[]{:S(2)}) copy-start(f32[96,768]{1,0:T(8,128)} %param.50) | copy-start | bytes 884740
  556.6 61.6 %copy-start.23 = (f32[96,768]{1,0:T(8,128)S(1)}, f32[96,768]{1,0:T(8,128)}, u32[]{:S(2)}) copy-start(f32[96,768]{1,0:T(8,128)} %param.51) | copy-start | bytes 884740
  595.5 47.6 %copy-start.1 = (bf16[768,768]{1,0:T(8,128)(2,1)S(1)}, bf16[768,768]{1,0:T(8,128)(2,1)}, u32[]{:S(2)}) copy-start(bf16[768,768]{1,0:T(8,128)(2,1)} %param.37) | copy-start | bytes 3538948
  (5 other events, 5.3 us)
Sparse Core Ops, SparseCore 0:
  32.7 33.7 all-gather.5
  68.9 24.0 all-gather.7
  94.9 38.9 all-gather.9
  135.6 38.9 all-gather.11
  333.3 35.0 reduce-scatter.14
  389.0 46.4 reduce-scatter.24
  439.3 54.1 reduce-scatter.16
  496.9 53.8 reduce-scatter.20
  553.8 19.3 reduce-scatter.26
  575.3 20.2 reduce-scatter.12
  597.8 20.3 reduce-scatter.18
  620.3 20.3 reduce-scatter.22
